TPU v7x, 128 devices: a whole 4x4x4 slice. The times are simulated.
128 devices in a mesh: heads: 8 (over z, core), width: 4 (over y), sae: 4 (over x).
Axes of the slice: x: 4, y: 4, z: 4, core: 2. Of those that a mesh axis runs over, the one named last changes fastest.
Arguments:
- x_in: bfloat16 [512, 4608], P(None, 'width'), may hold values from -64 to 64
- doc_lengths: int32 [4], replicated, may hold values from 1 to 256, 512 in all
- attn_gain: float32 [4608], P('width'), may hold values from 0.25 to 1.75
- w_query: bfloat16 [4608, 4096], P('width', 'heads'), may hold values from -0.09375 to 0.09375
- w_key: bfloat16 [4608, 2048], P('width', 'heads'), may hold values from -0.09375 to 0.09375
- w_value: bfloat16 [4608, 2048], P('width', 'heads'), may hold values from -0.09375 to 0.09375
- w_out: bfloat16 [4096, 4608], P('heads', 'width'), may hold values from -0.09375 to 0.09375
- post_gain: float32 [4608], replicated, may hold values from 0.25 to 1.75
- enc_weight: bfloat16 [4608, 65536], P(None, ('heads', 'width', 'sae')), may hold values from -0.09375 to 0.09375
- enc_bias: float32 [65536], P(('heads', 'width', 'sae')), may hold values from -1.5 to 0.5
- dec_weight: bfloat16 [65536, 4608], P(('heads', 'width', 'sae')), may hold values from -1 to 1
- dec_bias: float32 [4608], replicated, may hold values from -5 to 5
Outputs:
- grad_enc: bfloat16 [4608, 65536], P(None, ('heads', 'width', 'sae'))
- grad_dec: bfloat16 [65536, 4608], P(('heads', 'width', 'sae'))
- total_loss: float32 [], replicated
Inputs may be any that keep to these rules, and one draw needn't show every extreme that they name: `doc_lengths`: lengths of the 4 documents packed in order; they sum to 512.
All inputs are finite; a program needn't handle non-finite values.
Results may differ from a plain program's by a relative error of at most 0.02.
Values may be sent and summed in bfloat16 or wider, within the bound.
A program may use at most 128 MiB of HBM per device.

v0:
```python
import jax
import jax.numpy as jnp
from jax import lax
from jax.sharding import PartitionSpec as P

D = 4608
HEADS = 32
HEAD_DIM = 128
norm_eps = 1e-06
soft_cap = 50.0
rope_base = 10000.0
l1_weight = 3.0


def rotary(values, position):
    half_dim = values.shape[-1] // 2
    frequency = rope_base ** (-2.0 * jnp.arange(half_dim, dtype=jnp.float32) / values.shape[-1])
    angles = position.astype(jnp.float32)[:, None] * frequency[None, :]
    cosine_table = jnp.cos(angles)[:, None, :]
    sine_table = jnp.sin(angles)[:, None, :]
    first_half = values[..., :half_dim]
    second_half = values[..., half_dim:]
    return jnp.concatenate(
        [
            first_half * cosine_table - second_half * sine_table,
            second_half * cosine_table + first_half * sine_table,
        ],
        axis=-1,
    )


def attend_rows(query_rows, key_rows, value_rows, allowed_rows, scale):
    scores = (
        jnp.einsum("tkgd,skd->kgts", query_rows, key_rows, preferred_element_type=jnp.float32)
        * scale
    )
    capped = soft_cap * jnp.tanh(scores / soft_cap)
    weights = jnp.where(allowed_rows[None, None], jnp.exp(capped), 0.0)
    totals = jnp.sum(weights, axis=-1, keepdims=True)
    probs_bf = (weights / totals).astype(jnp.bfloat16)
    return jnp.einsum(
        "kgts,skd->tkgd", probs_bf, value_rows, preferred_element_type=jnp.float32
    ).astype(jnp.bfloat16)


def per_device(
    x_in,
    doc_lengths,
    attn_gain,
    w_query,
    w_key,
    w_value,
    w_out,
    post_gain,
    enc_weight,
    enc_bias,
    dec_weight,
    dec_bias,
):
    tokens = x_in.shape[0]
    query_heads = w_query.shape[1] // HEAD_DIM
    value_heads = w_key.shape[1] // HEAD_DIM
    boundary = jnp.cumsum(doc_lengths)
    position = jnp.arange(tokens, dtype=jnp.int32)
    segment = jnp.sum((boundary[None, :] <= position[:, None]).astype(jnp.int32), axis=1)
    allowed = (segment[:, None] == segment[None, :]) & (position[None, :] <= position[:, None])
    x_float = x_in.astype(jnp.float32)
    scaled = (x_float * attn_gain).astype(jnp.bfloat16)
    query_part = jnp.dot(scaled, w_query, preferred_element_type=jnp.float32)
    key_part = jnp.dot(scaled, w_key, preferred_element_type=jnp.float32)
    value_part = jnp.dot(scaled, w_value, preferred_element_type=jnp.float32)
    square_part = jnp.sum(x_float * x_float, axis=1)
    query_raw, key_raw, value_raw, square_sums = lax.psum(
        (query_part, key_part, value_part, square_part), "width"
    )
    inverse_rms = lax.rsqrt(square_sums / D + norm_eps)
    query = rotary(
        (query_raw * inverse_rms[:, None]).reshape(tokens, query_heads, HEAD_DIM), position
    ).astype(jnp.bfloat16)
    key_rows = rotary(
        (key_raw * inverse_rms[:, None]).reshape(tokens, value_heads, HEAD_DIM), position
    ).astype(jnp.bfloat16)
    value_rows = (
        (value_raw * inverse_rms[:, None])
        .reshape(tokens, value_heads, HEAD_DIM)
        .astype(jnp.bfloat16)
    )
    query4 = query.reshape(tokens, value_heads, query_heads // value_heads, HEAD_DIM)
    pieces_out = attend_rows(query4, key_rows, value_rows, allowed, (D // HEADS) ** (-0.5))
    mixed = pieces_out.reshape(tokens, query_heads * HEAD_DIM)
    proj_part = jnp.dot(mixed, w_out, preferred_element_type=jnp.float32)
    attn_sum = lax.psum(proj_part, "heads")
    attn_local = attn_sum.astype(jnp.bfloat16)
    attn_proj, x_full = (
        lax.all_gather(attn_local, "width", axis=1, tiled=True),
        lax.all_gather(x_in, "width", axis=1, tiled=True),
    )
    proj_float = attn_proj.astype(jnp.float32)
    inverse_post = lax.rsqrt(jnp.sum(proj_float * proj_float, axis=1) / D + norm_eps)
    resid = (x_full.astype(jnp.float32) + proj_float * inverse_post[:, None] * post_gain).astype(
        jnp.bfloat16
    )
    centered = (resid.astype(jnp.float32) - dec_bias).astype(jnp.bfloat16)
    pre_acts = jnp.dot(centered, enc_weight, preferred_element_type=jnp.float32) + enc_bias
    latent_acts = jnp.maximum(pre_acts, 0.0).astype(jnp.bfloat16)
    row_norms = jnp.sqrt(jnp.sum(jnp.square(dec_weight.astype(jnp.float32)), axis=1) + norm_eps)
    act_sums = jnp.sum(latent_acts.astype(jnp.float32), axis=0)
    penalty_part = jnp.sum(act_sums * row_norms)
    recon_part = jnp.dot(latent_acts, dec_weight, preferred_element_type=jnp.float32)
    recon = lax.psum(recon_part, ("heads", "width", "sae")) + dec_bias
    error = recon - resid.astype(jnp.float32)
    squares_total = jnp.sum(error * error)
    penalty_total = lax.psum(penalty_part, ("heads", "width", "sae"))
    grad_recon = (2.0 / tokens * error).astype(jnp.bfloat16)
    total_loss = (squares_total + l1_weight * penalty_total) / (tokens * D)
    upstream = lax.dot_general(
        grad_recon, dec_weight, (((1,), (1,)), ((), ())), preferred_element_type=jnp.float32
    )
    grad_pre = jnp.where(pre_acts > 0, upstream + l1_weight * row_norms / tokens, 0.0).astype(
        jnp.bfloat16
    )
    grad_enc = lax.dot_general(
        centered, grad_pre, (((0,), (0,)), ((), ())), preferred_element_type=jnp.float32
    ).astype(jnp.bfloat16)
    decoder_term = lax.dot_general(
        latent_acts, grad_recon, (((0,), (0,)), ((), ())), preferred_element_type=jnp.float32
    )
    grad_dec = (
        decoder_term
        + l1_weight
        / tokens
        * act_sums[:, None]
        * dec_weight.astype(jnp.float32)
        / row_norms[:, None]
    ).astype(jnp.bfloat16)
    return (grad_enc, grad_dec, total_loss)


def solution(mesh):
    placed = (
        P(None, "width"),
        P(),
        P("width"),
        P("width", "heads"),
        P("width", "heads"),
        P("width", "heads"),
        P("heads", "width"),
        P(),
        P(None, ("heads", "width", "sae")),
        P(("heads", "width", "sae")),
        P(("heads", "width", "sae"), None),
        P(),
    )
    return jax.shard_map(
        per_device,
        mesh=mesh,
        in_specs=placed,
        out_specs=(P(None, ("heads", "width", "sae")), P(("heads", "width", "sae"), None), P()),
        check_vma=False,
    )
```

profile of v0, /device:TPU:1, one launch (start us, length us, event | category | flops | bytes accessed | tf_op | source)
XLA Modules:
  0.0 471.6 jit_solution(9375944868353371698)
XLA Ops:
  7.2 0.0 copy-start
  7.2 0.0 all-reduce.7.cloned.1.call-start
  7.3 3.6 fusion.23
  10.9 2.7 fusion.25
  13.6 1.3 fusion.27
  14.9 0.0 all-reduce.7.cloned.1.call-update
  15.0 0.0 all-gather.5.cloned.1.call-start
  15.0 0.2 reduce-window.8
  15.2 0.3 fusion.14
  15.5 9.5 %psum.50 = f32[512]{0:T(512)S(1)} all-reduce(f32[512]{0:T(512)S(1)} %fusion.14), channel_id=1, replica_groups=mesh['heads'=8,'width'=4,'sae'=4] {'width'}, use_global_device_ids=true, to_apply=%region_2.3 | all-reduce | flops 512 | bytes 4096 | tf_op jit(solution)/shard_map/psum | solution.py:73
  25.1 0.1 convert_reduce_fusion.1
  25.2 0.9 fusion.22
  26.1 1.7 multiply_cosine_fusion
  27.8 49.0 %all-reduce.7.cloned.1.call-done = (f32[512,256]{1,0:T(8,128)}, f32[512,512]{1,0:T(8,128)}, f32[512,256]{1,0:T(8,128)}) async-done(((f32[512,256]{1,0:T(8,128)}, f32[512,512]{1,0:T(8,128)}, f32[512,256]{1,0:T(8,128)}), (f32[512,256]{1,0:T(8,128)}, f32[512,512]{1,0:T(8,128)}, f32[512,256]{1,0:T(8,128)})) %all-reduce.7.cloned.1.call-update) | async-done | bytes 2097168 | tf_op jit(solution)/shard_map/psum | solution.py:73
  76.9 2.1 broadcast_multiply_fusion.1
  78.9 0.3 reshape.168
  79.2 1.5 fusion.40
  80.7 1.4 broadcast_multiply_fusion
  82.1 0.4 reshape.169
  82.5 1.8 subtract_convert_fusion
  84.3 0.1 copy.23
  84.3 0.1 copy.24
  84.4 0.1 copy.30
  84.6 1.3 subtract_convert_fusion.1
  85.9 2.9 fusion.12
  88.8 1.6 fusion.21
  90.4 0.9 fusion.41
  91.3 52.5 %all-reduce.8 = bf16[512,1152]{1,0:T(8,128)(2,1)} all-reduce(f32[512,1152]{1,0:T(8,128)S(1)} %fusion.41), channel_id=1, replica_groups=mesh['heads'=8,'width'=4,'sae'=4] {'heads'}, use_global_device_ids=true, to_apply=%region_8.9 | all-reduce | flops 589824 | bytes 3538944 | tf_op jit(solution)/shard_map/psum | solution.py:92
  143.8 0.0 all-gather.5.cloned.1.call-update
  143.8 0.0 all-gather.3.cloned.1.call-start
  143.8 0.7 all-gather.3.cloned.1.call-update
  144.5 0.2 all-reduce.5.cloned.1.call-start
  144.8 51.8 %all-gather.5.cloned.1.call-done = bf16[512,4608]{1,0:T(8,128)(2,1)} async-done(((bf16[512,1152]{1,0:T(8,128)(2,1)}), bf16[512,4608]{1,0:T(8,128)(2,1)}) %all-gather.5.cloned.1.call-update) | async-done | bytes 4718608 | tf_op jit(solution)/shard_map/all_gather | solution.py:95
  196.6 3.3 fusion
  200.0 51.3 %all-gather.3.cloned.1.call-done = bf16[512,4608]{1,0:T(8,128)(2,1)} async-done(((bf16[512,1152]{1,0:T(8,128)(2,1)}), bf16[512,4608]{1,0:T(8,128)(2,1)}) %all-gather.3.cloned.1.call-update) | async-done | bytes 4718608 | tf_op jit(solution)/shard_map/all_gather | solution.py:96
  251.3 5.9 %fusion.3 = bf16[512,4608]{1,0:T(8,128)(2,1)S(1)} fusion(bf16[512,4608]{1,0:T(8,128)(2,1)} %all-gather.5.cloned.1.call-done, bf16[512,4608]{1,0:T(8,128)(2,1)} %all-gather.3.cloned.1.call-done, f32[4608]{0:T(1024)S(1)} %copy-done.8, f32[512]{0:T(512)S(1)} %add_rsqrt_fusion), kind=kLoop, calls=%fused_computation.9 | loop fusion | flops 14155776 | bytes 14176256 | tf_op jit(solution)/shard_map/convert_element_type | solution.py:100
  257.2 0.0 slice-start.1
  257.3 6.4 %convert_reduce_fusion = (f32[512]{0:T(512)S(1)}, f32[512,512]{1,0:T(8,128)S(1)}) fusion(f32[512]{0:T(512)S(1)} %copy-done.12, bf16[4608,512]{1,0:T(8,128)(2,1)} %param.20, bf16[512,4608]{1,0:T(8,128)(2,1)S(1)} %fusion.3, f32[4608]{0:T(1024)S(1)} %copy-done.9), kind=kOutput, calls=%fused_computation.32 | convolution fusion | flops 2424045056 | bytes 10508288 | tf_op jit(solution)/shard_map/dot_general | solution.py:104
  263.7 5.1 %fusion.39 = f32[512,4608]{1,0:T(8,128)} fusion(bf16[512,4608]{1,0:T(8,128)(2,1)S(1)} %bitcast.41, f32[512,512]{1,0:T(8,128)S(1)} %get-tuple-element.25), kind=kOutput, calls=%fused_computation.69 | convolution fusion | flops 2416443392 | bytes 15204352 | tf_op jit(solution)/shard_map/dot_general | solution.py:109
  268.8 0.0 all-reduce.5.cloned.1.call-update
  268.8 3.3 fusion.5
  272.2 0.6 multiply_reduce_fusion.1
  272.8 65.8 %psum.55 = f32[]{:T(128)} all-reduce(f32[]{:T(128)} %get-tuple-element.16), channel_id=1, replica_groups=mesh['heads'=8,'width'=4,'sae'=4] {'heads','width','sae'}, use_global_device_ids=true, to_apply=%region_15.16 | all-reduce | flops 1 | bytes 8 | tf_op jit(solution)/shard_map/psum | solution.py:113
  339.2 94.4 %all-reduce.5.cloned.1.call-done = f32[512,4608]{1,0:T(8,128)} async-done(((f32[512,4608]{1,0:T(8,128)}), f32[512,4608]{1,0:T(8,128)}) %all-reduce.5.cloned.1.call-update) | async-done | bytes 9437200 | tf_op jit(solution)/shard_map/psum | solution.py:110
  433.6 8.4 %multiply_reduce_fusion = (f32[]{:T(128)}, bf16[512,4608]{1,0:T(8,128)(2,1)S(1)}) fusion(bf16[512,4608]{1,0:T(8,128)(2,1)} %copy-done.2, f32[512,4608]{1,0:T(8,128)} %all-reduce.5.cloned.1.call-done, f32[4608]{0:T(1024)S(1)} %copy-done.9), kind=kLoop, calls=%fused_computation.15 | loop fusion | flops 16515071 | bytes 18892804 | tf_op jit(solution)/shard_map/reduce_sum | solution.py:112
  442.0 6.7 %fusion.20 = bf16[512,512]{1,0:T(8,128)(2,1)S(1)} fusion(bf16[512,4608]{1,0:T(8,128)(2,1)S(1)} %get-tuple-element.7, bf16[512,4608]{1,0:T(8,128)(2,1)} %param.22, f32[512,512]{1,0:T(8,128)S(1)} %get-tuple-element.25, f32[512]{0:T(512)S(1)} %get-tuple-element.17), kind=kOutput, calls=%fused_computation.30 | convolution fusion | flops 2416967680 | bytes 11012096 | tf_op jit(solution)/shard_map/dot_general | solution.py:116
  448.7 6.8 %convolution_convert_fusion = bf16[4608,512]{1,0:T(8,128)(2,1)} fusion(bf16[512,512]{1,0:T(8,128)(2,1)S(1)} %fusion.20, bf16[512,4608]{1,0:T(8,128)(2,1)} %copy-done.2, f32[4608]{0:T(1024)S(1)} %copy-done.9), kind=kOutput, calls=%fused_computation.17 | convolution fusion | flops 2425356288 | bytes 9979904 | tf_op jit(solution)/shard_map/dot_general | solution.py:122
  456.1 7.8 %fusion.8 = bf16[512,4608]{1,0:T(8,128)(2,1)} fusion(bf16[512,4608]{1,0:T(8,128)(2,1)} %param.22, bf16[512,4608]{1,0:T(8,128)(2,1)} %copy-done.4, f32[512]{0:T(512)S(1)} %get-tuple-element.18, f32[512]{0:T(512)S(1)} %get-tuple-element.19, f32[512,512]{1,0:T(8,128)S(1)} %get-tuple-element.25), kind=kOutput, calls=%fused_computation.14 | convolution fusion | flops 2428239872 | bytes 15208448 | tf_op jit(solution)/shard_map/dot_general | solution.py:125
  (35 shorter events, 0.1 us)
Async XLA Ops:
  7.2 83.3 %copy-start = (bf16[512,1152]{1,0:T(8,128)(2,1)S(1)}, bf16[512,1152]{1,0:T(8,128)(2,1)}, u32[]{:S(2)}) copy-start(bf16[512,1152]{1,0:T(8,128)(2,1)} %param.18) | copy-start | bytes 3538948
  7.2 6.5 %copy-start.3 = (bf16[512,1152]{1,0:T(8,128)(2,1)S(1)}, bf16[512,1152]{1,0:T(8,128)(2,1)}, u32[]{:S(2)}) copy-start(bf16[512,1152]{1,0:T(8,128)(2,1)} %param.12) | copy-start | bytes 3538948
  7.2 6.4 %copy-start.11 = (f32[1152]{0:T(1024)S(1)}, f32[1152]{0:T(1024)}, u32[]{:S(2)}) copy-start(f32[1152]{0:T(1024)} %param.14) | copy-start | bytes 13828
  7.2 6.4 %copy-start.10 = (bf16[1152,256]{1,0:T(8,128)(2,1)S(1)}, bf16[1152,256]{1,0:T(8,128)(2,1)}, u32[]{:S(2)}) copy-start(bf16[1152,256]{1,0:T(8,128)(2,1)} %param.17) | copy-start | bytes 1769476
  7.2 7.8 %copy-start.13 = (s32[4]{0:T(128)S(1)}, s32[4]{0:T(128)}, u32[]{:S(2)}) copy-start(s32[4]{0:T(128)} %param.13) | copy-start | bytes 52
  7.2 69.6 %all-reduce.7.cloned.1.call-start = ((), (), s32[]{:S(2)}) async-start(), calls=%async_computation.3 | async-start | bytes 4194304 | tf_op jit(solution)/shard_map/psum | solution.py:73
  15.0 181.6 %all-gather.5.cloned.1.call-start = ((), (), s32[]{:S(2)}) async-start(), calls=%async_computation.1 | async-start | bytes 5898240 | tf_op jit(solution)/shard_map/all_gather | solution.py:95
  82.4 2.0 copy-start.6
  82.4 2.1 copy-start.5
  85.9 2.9 copy-start.7
  91.3 160.0 %copy-start.8 = (f32[4608]{0:T(1024)S(1)}, f32[4608]{0:T(1024)}, u32[]{:S(2)}) copy-start(f32[4608]{0:T(1024)} %param.19) | copy-start | bytes 55300
  143.8 107.5 %all-gather.3.cloned.1.call-start = ((), (), s32[]{:S(2)}) async-start(), calls=%async_computation | async-start | bytes 5898240 | tf_op jit(solution)/shard_map/all_gather | solution.py:96
  144.5 289.1 %all-reduce.5.cloned.1.call-start = ((), (), s32[]{:S(2)}) async-start(), calls=%async_computation.2 | async-start | bytes 18874368 | tf_op jit(solution)/shard_map/psum | solution.py:110
  199.9 57.3 %copy-start.9 = (f32[4608]{0:T(1024)S(1)}, f32[4608]{0:T(1024)}, u32[]{:S(2)}) copy-start(f32[4608]{0:T(1024)} %param.23) | copy-start | bytes 55300
  199.9 57.3 %copy-start.12 = (f32[512]{0:T(512)S(1)}, f32[512]{0:T(512)}, u32[]{:S(2)}) copy-start(f32[512]{0:T(512)} %param.21) | copy-start | bytes 6148
  251.3 12.4 %slice-start = ((s8[4718592]{0:T(1024)(128)(4,1)}), s8[4194304]{0:T(1024)(128)(4,1)S(1)}, s32[]{:S(2)}) async-start(s8[4718592]{0:T(1024)(128)(4,1)} %bitcast.40), calls=%async_computation.4 | async-start | bytes 8388608
  257.2 6.4 %copy-start.2 = (bf16[512,4608]{1,0:T(8,128)(2,1)}, bf16[512,4608]{1,0:T(8,128)(2,1)S(1)}, u32[]{:S(2)}) copy-start(bf16[512,4608]{1,0:T(8,128)(2,1)S(1)} %fusion.3) | copy-start | bytes 14155780
  257.2 6.5 %slice-start.1 = ((s8[4718592]{0:T(1024)(128)(4,1)}), s8[524288]{0:T(1024)(128)(4,1)S(1)}, s32[]{:S(2)}) async-start(s8[4718592]{0:T(1024)(128)(4,1)} %bitcast.40), calls=%async_computation.5 | async-start | bytes 1048576
  442.0 6.7 %copy-start.4 = (bf16[512,4608]{1,0:T(8,128)(2,1)}, bf16[512,4608]{1,0:T(8,128)(2,1)S(1)}, u32[]{:S(2)}) copy-start(bf16[512,4608]{1,0:T(8,128)(2,1)S(1)} %get-tuple-element.7) | copy-start | bytes 14155780
  456.1 7.9 %copy-start.1 = (bf16[512,1152]{1,0:T(8,128)(2,1)S(1)}, bf16[512,1152]{1,0:T(8,128)(2,1)}, u32[]{:S(2)}) copy-start(bf16[512,1152]{1,0:T(8,128)(2,1)} %param.18) | copy-start | bytes 3538948
Sparse Core Ops, SparseCore 0:
  15.1 61.7 all-reduce.6
  143.9 52.6 all-gather.4
  198.3 52.9 all-gather.2
  268.9 164.6 all-reduce.4
where the time goes:
time: 472 us
  waiting for transfers between devices  247 us (52%)
  blocking collectives  128 us (27%)
  matrix products  45.7 us (10%)
  other arithmetic  31.4 us (7%)
  between operations  16.5 us (3%)
    psum x1, waiting for transfers between devices, per_device(): recon = lax.psum(recon_part, ('heads', 'width', 'sae')) + dec_bias  94.4 us
    psum x1, blocking collectives, per_device(): penalty_total = lax.psum(penalty_part, ('heads', 'width', 'sae'))  65.8 us
    psum x1, blocking collectives, per_device(): attn_sum = lax.psum(proj_part, 'heads')  52.5 us
    all_gather x1, waiting for transfers between devices, per_device(): lax.all_gather(attn_local, 'width', axis=1, tiled=True)  51.8 us
    all_gather x1, waiting for transfers between devices, per_device(): lax.all_gather(x_in, 'width', axis=1, tiled=True)  51.3 us
    psum x1, waiting for transfers between devices, per_device(): lax.psum((query_part, key_part, value_part, square_part), 'width')  49 us
    psum x1, blocking collectives, per_device(): lax.psum((query_part, key_part, value_part, square_part), 'width')  9.54 us
  transfers between devices with their start and end apart: 4, of which 4 were waited for; matrix products, arithmetic and copies ran while one was open for 2% of the time, Pallas kernels for 0%

commit v1 on v0

--- a/solution.py
+++ b/solution.py
@@ -10,6 +10,18 @@
 soft_cap = 50.0
 rope_base = 10000.0
 l1_weight = 3.0
+
+
+def _play_core(payload):
+    return jnp.concatenate(
+        lax.all_to_all(
+            jnp.stack(tuple((payload for _ in range(lax.axis_size("width"))))),
+            axis_name="width",
+            split_axis=0,
+            concat_axis=0,
+        ),
+        1,
+    )
 
 
 def rotary(values, position):
@@ -91,10 +103,7 @@
     proj_part = jnp.dot(mixed, w_out, preferred_element_type=jnp.float32)
     attn_sum = lax.psum(proj_part, "heads")
     attn_local = attn_sum.astype(jnp.bfloat16)
-    attn_proj, x_full = (
-        lax.all_gather(attn_local, "width", axis=1, tiled=True),
-        lax.all_gather(x_in, "width", axis=1, tiled=True),
-    )
+    attn_proj, x_full = (_play_core(attn_local), lax.all_gather(x_in, "width", axis=1, tiled=True))
     proj_float = attn_proj.astype(jnp.float32)
     inverse_post = lax.rsqrt(jnp.sum(proj_float * proj_float, axis=1) / D + norm_eps)
     resid = (x_full.astype(jnp.float32) + proj_float * inverse_post[:, None] * post_gain).astype(

time: 472 us -> 430 us (0.911)
  waiting for transfers between devices: 247 us -> 142 us
  blocking collectives: 128 us -> 186 us
  local copies, waits for them, and re-layouts: 2.52 us -> 7.77 us
    all_to_all x0 -> x1, blocking collectives: none -> 53.3 us  [_play_core(): lax.all_to_all(jnp.stack(tuple((payload for _ in range(lax.axis_size('wid...]
    all_gather x1 -> x0, waiting for transfers between devices: 51.8 us -> none  [per_device(): lax.all_gather(attn_local, 'width', axis=1, tiled=True)]
    all_gather x1, waiting for transfers between devices: 51.3 us -> 0.02 us  [per_device(): lax.all_gather(x_in, 'width', axis=1, tiled=True)]
    convert_element_type x0 -> x1, local copies, waits for them, and re-layouts: none -> 4.9 us  [per_device(): proj_float = attn_proj.astype(jnp.float32)]
  transfers between devices with their start and end apart: 4 -> 3, of which waited for: 4 -> 2; matrix products, arithmetic and copies ran while one was open for 2% -> 7% of each run, Pallas kernels for 0% -> 0%
where the time goes in v1:
time: 430 us; the launch traced here: 429 us
  blocking collectives  186 us (43%)
  waiting for transfers between devices  142 us (33%)
  matrix products  45.8 us (11%)
  other arithmetic  30.7 us (7%)
  between operations  16.5 us (4%)
  local copies, waits for them, and re-layouts  7.77 us (2%)
    psum x1, waiting for transfers between devices, per_device(): recon = lax.psum(recon_part, ('heads', 'width', 'sae')) + dec_bias  92.8 us
    psum x1, blocking collectives, per_device(): penalty_total = lax.psum(penalty_part, ('heads', 'width', 'sae'))  69.7 us
    psum x1, blocking collectives, per_device(): attn_sum = lax.psum(proj_part, 'heads')  53.8 us
    all_to_all x1, blocking collectives, _play_core(): lax.all_to_all(jnp.stack(tuple((payload for _ in range(lax.axis_size('wid...  53.3 us
    psum x1, waiting for transfers between devices, per_device(): lax.psum((query_part, key_part, value_part, square_part), 'width')  48.3 us
    psum x1, blocking collectives, per_device(): lax.psum((query_part, key_part, value_part, square_part), 'width')  9.55 us
  transfers between devices with their start and end apart: 3, of which 2 were waited for; matrix products, arithmetic and copies ran while one was open for 7% of the time, Pallas kernels for 0%

profile of v1, /device:TPU:1, one launch (start us, length us, event | category | flops | bytes accessed | tf_op | source)
XLA Modules:
  0.0 429.2 jit_solution(10197811682209473873)
XLA Ops:
  7.2 0.0 copy-start
  7.2 0.0 all-reduce.7.cloned.1.call-start
  7.3 3.6 fusion.20
  10.9 2.8 fusion.22
  13.7 1.3 fusion.24
  15.0 0.0 all-reduce.7.cloned.1.call-update
  15.1 0.0 all-gather.2.cloned.1.call-start
  15.1 0.7 all-gather.2.cloned.1.call-update
  15.8 0.0 all-reduce.5.cloned.1.call-start
  15.9 0.3 fusion.11
  16.2 9.5 %psum.50 = f32[512]{0:T(512)S(1)} all-reduce(f32[512]{0:T(512)S(1)} %fusion.11), channel_id=1, replica_groups=mesh['heads'=8,'width'=4,'sae'=4] {'width'}, use_global_device_ids=true, to_apply=%region_2.3 | all-reduce | flops 512 | bytes 4096 | tf_op jit(solution)/shard_map/psum | solution.py:85
  25.8 0.2 reduce-window.8
  25.9 0.1 convert_reduce_fusion.1
  26.0 0.9 fusion.19
  26.9 1.7 multiply_cosine_fusion
  28.7 48.3 %all-reduce.7.cloned.1.call-done = (f32[512,256]{1,0:T(8,128)}, f32[512,512]{1,0:T(8,128)}, f32[512,256]{1,0:T(8,128)}) async-done(((f32[512,256]{1,0:T(8,128)}, f32[512,512]{1,0:T(8,128)}, f32[512,256]{1,0:T(8,128)}), (f32[512,256]{1,0:T(8,128)}, f32[512,512]{1,0:T(8,128)}, f32[512,256]{1,0:T(8,128)})) %all-reduce.7.cloned.1.call-update) | async-done | bytes 2097168 | tf_op jit(solution)/shard_map/psum | solution.py:85
  76.9 2.1 broadcast_multiply_fusion.1
  79.0 0.3 reshape.174
  79.3 1.5 fusion.37
  80.8 1.4 broadcast_multiply_fusion
  82.2 0.4 reshape.175
  82.6 1.8 subtract_convert_fusion
  84.4 0.1 copy.30
  84.4 0.1 copy.31
  84.5 0.1 copy.38
  84.7 1.3 subtract_convert_fusion.1
  86.0 2.9 fusion.9
  88.9 1.6 fusion.18
  90.5 0.9 fusion.38
  91.4 53.8 %all-reduce.8 = bf16[512,1152]{1,0:T(8,128)(2,1)S(1)} all-reduce(f32[512,1152]{1,0:T(8,128)S(1)} %fusion.38), channel_id=1, replica_groups=mesh['heads'=8,'width'=4,'sae'=4] {'heads'}, use_global_device_ids=true, to_apply=%region_8.9 | all-reduce | flops 589824 | bytes 3538944 | tf_op jit(solution)/shard_map/psum | solution.py:104
  145.2 0.3 stack.2
  145.6 53.3 %all_to_all.5 = bf16[4,512,1152]{2,1,0:T(8,128)(2,1)S(1)} all-to-all(bf16[4,512,1152]{2,1,0:T(8,128)(2,1)S(1)} %stack.2), channel_id=1, replica_groups=mesh['heads'=8,'width'=4,'sae'=4] {'width'}, dimensions={0} | all-to-all | bytes 9437184 | tf_op jit(solution)/shard_map/all_to_all | solution.py:17
  198.9 0.6 convert_bitcast_fusion
  199.5 4.9 %copy.41 = f32[4,64,8,1152]{3,2,0,1:T(8,128)} copy(f32[4,64,8,1152]{3,2,1,0:T(8,128)S(1)} %convert_bitcast_fusion) | data formatting | bytes 18874368 | tf_op jit(solution)/shard_map/convert_element_type | solution.py:107
  204.4 1.0 fusion.5
  205.4 0.0 all-gather.2.cloned.1.call-done
  205.5 6.9 %add_convert_fusion = bf16[512,4608]{1,0:T(8,128)(2,1)S(1)} fusion(f32[512,4608]{1,0:T(8,128)} %bitcast.44, bf16[512,4608]{1,0:T(8,128)(2,1)} %all-gather.2.cloned.1.call-done, f32[4608]{0:T(1024)S(1)} %copy-done.9, f32[512]{0:T(512)S(1)} %add_rsqrt_fusion), kind=kLoop, calls=%fused_computation.14 | loop fusion | flops 11796480 | bytes 18894848 | tf_op jit(solution)/shard_map/convert_element_type | solution.py:109
  212.5 6.5 %convert_reduce_fusion = (f32[512]{0:T(512)S(1)}, f32[512,512]{1,0:T(8,128)S(1)}) fusion(f32[512]{0:T(512)S(1)} %copy-done.13, bf16[4608,512]{1,0:T(8,128)(2,1)} %param.20, bf16[512,4608]{1,0:T(8,128)(2,1)S(1)} %add_convert_fusion, f32[4608]{0:T(1024)S(1)} %copy-done.10), kind=kOutput, calls=%fused_computation.30 | convolution fusion | flops 2424045056 | bytes 10508288 | tf_op jit(solution)/shard_map/dot_general | solution.py:113
  219.0 5.1 %fusion.36 = f32[512,4608]{1,0:T(8,128)} fusion(bf16[512,4608]{1,0:T(8,128)(2,1)S(1)} %bitcast.46, f32[512,512]{1,0:T(8,128)S(1)} %get-tuple-element.25), kind=kOutput, calls=%fused_computation.67 | convolution fusion | flops 2416443392 | bytes 15204352 | tf_op jit(solution)/shard_map/dot_general | solution.py:118
  224.1 0.0 all-reduce.5.cloned.1.call-update
  224.1 3.3 fusion.1
  227.4 0.6 multiply_reduce_fusion.1
  228.0 69.7 %psum.55 = f32[]{:T(128)} all-reduce(f32[]{:T(128)} %get-tuple-element.16), channel_id=1, replica_groups=mesh['heads'=8,'width'=4,'sae'=4] {'heads','width','sae'}, use_global_device_ids=true, to_apply=%region_15.16 | all-reduce | flops 1 | bytes 8 | tf_op jit(solution)/shard_map/psum | solution.py:122
  298.4 92.8 %all-reduce.5.cloned.1.call-done = f32[512,4608]{1,0:T(8,128)} async-done(((f32[512,4608]{1,0:T(8,128)}), f32[512,4608]{1,0:T(8,128)}) %all-reduce.5.cloned.1.call-update) | async-done | bytes 9437200 | tf_op jit(solution)/shard_map/psum | solution.py:119
  391.2 8.4 %multiply_reduce_fusion = (f32[]{:T(128)}, bf16[512,4608]{1,0:T(8,128)(2,1)S(1)}) fusion(bf16[512,4608]{1,0:T(8,128)(2,1)} %copy-done.2, f32[512,4608]{1,0:T(8,128)} %all-reduce.5.cloned.1.call-done, f32[4608]{0:T(1024)S(1)} %copy-done.10), kind=kLoop, calls=%fused_computation.12 | loop fusion | flops 16515071 | bytes 18892804 | tf_op jit(solution)/shard_map/reduce_sum | solution.py:121
  399.6 6.7 %fusion.17 = bf16[512,512]{1,0:T(8,128)(2,1)S(1)} fusion(bf16[512,4608]{1,0:T(8,128)(2,1)S(1)} %get-tuple-element.7, bf16[512,4608]{1,0:T(8,128)(2,1)} %param.22, f32[512,512]{1,0:T(8,128)S(1)} %get-tuple-element.25, f32[512]{0:T(512)S(1)} %get-tuple-element.17), kind=kOutput, calls=%fused_computation.28 | convolution fusion | flops 2416967680 | bytes 11012096 | tf_op jit(solution)/shard_map/dot_general | solution.py:125
  406.3 6.7 %convolution_convert_fusion = bf16[4608,512]{1,0:T(8,128)(2,1)} fusion(bf16[512,512]{1,0:T(8,128)(2,1)S(1)} %fusion.17, bf16[512,4608]{1,0:T(8,128)(2,1)} %copy-done.2, f32[4608]{0:T(1024)S(1)} %copy-done.10), kind=kOutput, calls=%fused_computation.15 | convolution fusion | flops 2425356288 | bytes 9979904 | tf_op jit(solution)/shard_map/dot_general | solution.py:131
  413.7 7.8 %fusion.4 = bf16[512,4608]{1,0:T(8,128)(2,1)} fusion(bf16[512,4608]{1,0:T(8,128)(2,1)} %param.22, bf16[512,4608]{1,0:T(8,128)(2,1)} %copy-done.5, f32[512]{0:T(512)S(1)} %get-tuple-element.18, f32[512]{0:T(512)S(1)} %get-tuple-element.19, f32[512,512]{1,0:T(8,128)S(1)} %get-tuple-element.25), kind=kOutput, calls=%fused_computation.10 | convolution fusion | flops 2428239872 | bytes 15208448 | tf_op jit(solution)/shard_map/dot_general | solution.py:134
  (38 shorter events, 0.1 us)
Async XLA Ops:
  7.2 83.4 %copy-start = (bf16[512,1152]{1,0:T(8,128)(2,1)S(1)}, bf16[512,1152]{1,0:T(8,128)(2,1)}, u32[]{:S(2)}) copy-start(bf16[512,1152]{1,0:T(8,128)(2,1)} %param.18) | copy-start | bytes 3538948
  7.2 6.5 %copy-start.3 = (bf16[512,1152]{1,0:T(8,128)(2,1)S(1)}, bf16[512,1152]{1,0:T(8,128)(2,1)}, u32[]{:S(2)}) copy-start(bf16[512,1152]{1,0:T(8,128)(2,1)} %param.12) | copy-start | bytes 3538948
  7.2 6.5 %copy-start.12 = (f32[1152]{0:T(1024)S(1)}, f32[1152]{0:T(1024)}, u32[]{:S(2)}) copy-start(f32[1152]{0:T(1024)} %param.14) | copy-start | bytes 13828
  7.2 69.7 %all-reduce.7.cloned.1.call-start = ((), (), s32[]{:S(2)}) async-start(), calls=%async_computation.3 | async-start | bytes 4194304 | tf_op jit(solution)/shard_map/psum | solution.py:85
  7.3 6.5 %copy-start.11 = (bf16[1152,256]{1,0:T(8,128)(2,1)S(1)}, bf16[1152,256]{1,0:T(8,128)(2,1)}, u32[]{:S(2)}) copy-start(bf16[1152,256]{1,0:T(8,128)(2,1)} %param.17) | copy-start | bytes 1769476
  10.9 5.0 %copy-start.4 = (bf16[512,1152]{1,0:T(8,128)(2,1)S(1)}, bf16[512,1152]{1,0:T(8,128)(2,1)}, u32[]{:S(2)}) copy-start(bf16[512,1152]{1,0:T(8,128)(2,1)} %param.12) | copy-start | bytes 3538948
  10.9 14.9 %copy-start.14 = (s32[4]{0:T(128)S(1)}, s32[4]{0:T(128)}, u32[]{:S(2)}) copy-start(s32[4]{0:T(128)} %param.13) | copy-start | bytes 52
  15.1 190.4 %all-gather.2.cloned.1.call-start = ((), (), s32[]{:S(2)}) async-start(), calls=%async_computation.1 | async-start | bytes 5898240 | tf_op jit(solution)/shard_map/all_gather | solution.py:106
  15.8 375.4 %all-reduce.5.cloned.1.call-start = ((), (), s32[]{:S(2)}) async-start(), calls=%async_computation.2 | async-start | bytes 18874368 | tf_op jit(solution)/shard_map/psum | solution.py:119
  82.5 2.0 copy-start.7
  82.5 2.1 copy-start.6
  86.0 2.9 copy-start.8
  204.4 1.0 copy-start.9
  205.5 7.0 %copy-start.10 = (f32[4608]{0:T(1024)S(1)}, f32[4608]{0:T(1024)}, u32[]{:S(2)}) copy-start(f32[4608]{0:T(1024)} %param.23) | copy-start | bytes 55300
  205.5 7.0 %copy-start.13 = (f32[512]{0:T(512)S(1)}, f32[512]{0:T(512)}, u32[]{:S(2)}) copy-start(f32[512]{0:T(512)} %param.21) | copy-start | bytes 6148
  205.5 13.5 %slice-start = ((s8[4718592]{0:T(1024)(128)(4,1)}), s8[524288]{0:T(1024)(128)(4,1)S(1)}, s32[]{:S(2)}) async-start(s8[4718592]{0:T(1024)(128)(4,1)} %bitcast.45), calls=%async_computation.4 | async-start | bytes 1048576
  212.5 6.5 %copy-start.2 = (bf16[512,4608]{1,0:T(8,128)(2,1)}, bf16[512,4608]{1,0:T(8,128)(2,1)S(1)}, u32[]{:S(2)}) copy-start(bf16[512,4608]{1,0:T(8,128)(2,1)S(1)} %add_convert_fusion) | copy-start | bytes 14155780
  212.5 6.5 %slice-start.1 = ((s8[4718592]{0:T(1024)(128)(4,1)}), s8[4194304]{0:T(1024)(128)(4,1)S(1)}, s32[]{:S(2)}) async-start(s8[4718592]{0:T(1024)(128)(4,1)} %bitcast.45), calls=%async_computation.5 | async-start | bytes 8388608
  399.6 6.7 %copy-start.5 = (bf16[512,4608]{1,0:T(8,128)(2,1)}, bf16[512,4608]{1,0:T(8,128)(2,1)S(1)}, u32[]{:S(2)}) copy-start(bf16[512,4608]{1,0:T(8,128)(2,1)S(1)} %get-tuple-element.7) | copy-start | bytes 14155780
  413.7 7.9 %copy-start.1 = (bf16[512,1152]{1,0:T(8,128)(2,1)S(1)}, bf16[512,1152]{1,0:T(8,128)(2,1)}, u32[]{:S(2)}) copy-start(bf16[512,1152]{1,0:T(8,128)(2,1)} %param.18) | copy-start | bytes 3538948
Sparse Core Ops, SparseCore 0:
  15.2 61.7 all-reduce.6
  78.6 52.3 all-gather.1
  224.2 166.9 all-reduce.4
